TPU v7x, 32 devices: a whole 2x2x4 slice. The times are simulated.
32 devices in a mesh: fsdp: 8 (over y, x, core), tp: 4 (over z).
Axes of the slice: x: 2, y: 2, z: 4, core: 2. Of those that a mesh axis runs over, the one named last changes fastest.
Arguments:
- inputs: bfloat16 [32, 448, 768], P(('fsdp', 'tp')), may hold values from -6 to 6
- encoder: bfloat16 [32, 1500, 768], P('fsdp', 'tp'), may hold values from -6 to 6
- lengths: int32 [32], P('fsdp'), may hold values from 56 to 448, as said below
- self_qkv: bfloat16 [3, 768, 768], P(None, 'fsdp', 'tp'), may hold values from -0.21875 to 0.21875
- self_out: bfloat16 [768, 768], P('tp', 'fsdp'), may hold values from -0.875 to 0.875
- cross_q: bfloat16 [768, 768], P('fsdp', 'tp'), may hold values from -0.21875 to 0.21875
- cross_kv: bfloat16 [2, 768, 768], P(None, 'fsdp', 'tp'), may hold values from -0.21875 to 0.21875
- cross_out: bfloat16 [768, 768], P('tp', 'fsdp'), may hold values from -1.25 to 1.25
- fc_in: bfloat16 [768, 3072], P('fsdp', 'tp'), may hold values from -0.21875 to 0.21875
- fc_out: bfloat16 [3072, 768], P('tp', 'fsdp'), may hold values from -0.109375 to 0.109375
- norm_gain: float32 [4, 768], P(None, ('fsdp', 'tp')), may hold values from 0.5 to 1.5
- norm_bias: float32 [4, 768], P(None, ('fsdp', 'tp')), may hold values from -4 to 4
- proj_bias: float32 [7, 768], P(None, ('fsdp', 'tp')), may hold values from -4 to 4
- fc_in_bias: float32 [3072], P(('fsdp', 'tp')), may hold values from -4 to 4
- cotangent: bfloat16 [32, 448, 768], P(('fsdp', 'tp')), may hold values from -6 to 6
Outputs:
- layer_out: bfloat16 [32, 448, 768], P(('fsdp', 'tp'))
- grad_inputs: float32 [32, 448, 768], P(('fsdp', 'tp'))
- grad_encoder: float32 [32, 1500, 768], P('fsdp', 'tp')
- grad_self_qkv: float32 [3, 768, 768], P(None, 'fsdp', 'tp')
- grad_self_out: float32 [768, 768], P('tp', 'fsdp')
- grad_cross_q: float32 [768, 768], P('fsdp', 'tp')
- grad_cross_kv: float32 [2, 768, 768], P(None, 'fsdp', 'tp')
- grad_cross_out: float32 [768, 768], P('tp', 'fsdp')
- grad_fc_in: float32 [768, 3072], P('fsdp', 'tp')
- grad_fc_out: float32 [3072, 768], P('tp', 'fsdp')
- grad_norm_gain: float32 [4, 768], P(None, ('fsdp', 'tp'))
- grad_norm_bias: float32 [4, 768], P(None, ('fsdp', 'tp'))
- grad_proj_bias: float32 [7, 768], P(None, ('fsdp', 'tp'))
- grad_fc_in_bias: float32 [3072], P(('fsdp', 'tp'))
Inputs may be any that keep to these rules, and one draw needn't show every extreme that they name: `lengths`: valid tokens of each sequence; later positions are padding and never serve as keys.
All inputs are finite; a program needn't handle non-finite values.
Results may differ from a plain program's by a relative error of at most 0.035.
Values may be sent and summed in bfloat16 or wider, within the bound.
No kernel may reach another device: no remote copies, remote signals or barrier semaphores. Data moves between devices by JAX's collectives and lax.ppermute only.
A program may use at most 192 MiB of HBM per device.

v0:
```python
import jax
import jax.numpy as jnp
from jax import lax
from jax.sharding import PartitionSpec as P

HD = 64
EPSILON = 1e-05
NEGATIVE = -1e30


def normalize(row_block, gain_row, shift_row):
    center = row_block - jnp.mean(row_block, -1, keepdims=True)
    inverse = lax.rsqrt(jnp.mean(center * center, -1, keepdims=True) + EPSILON)
    unit_rows = center * inverse
    return (unit_rows * gain_row + shift_row, unit_rows, inverse)


def norm_back(grad_rows, unit_rows, inverse, gain_row):
    scaled = grad_rows * gain_row
    return inverse * (
        scaled
        - jnp.mean(scaled, -1, keepdims=True)
        - unit_rows * jnp.mean(scaled * unit_rows, -1, keepdims=True)
    )


def matmul(left_side, right_side):
    return jnp.dot(left_side, right_side, preferred_element_type=jnp.float32)


def transposed(left_side, right_side):
    return lax.dot_general(
        left_side, right_side, (((0,), (0,)), ((), ())), preferred_element_type=jnp.float32
    )


def against(left_side, right_side):
    return lax.dot_general(
        left_side, right_side, (((1,), (1,)), ((), ())), preferred_element_type=jnp.float32
    )


def exact_gelu(values):
    return jax.nn.gelu(values, approximate=False)


def row_sum(values):
    return jnp.sum(values.reshape(-1, values.shape[-1]), 0)


def attend_forward(query_seq, key_seq, value_seq, allowed):
    scores = jnp.einsum("qhd,khd->hqk", query_seq, key_seq, preferred_element_type=jnp.float32)
    if allowed is not None:
        scores = jnp.where(allowed[None], scores, NEGATIVE)
    highest = jnp.max(scores, -1, keepdims=True)
    shifted = jnp.exp(scores - highest)
    total = jnp.sum(shifted, -1, keepdims=True)
    weights = (shifted / total).astype(jnp.bfloat16)
    output = jnp.einsum("hqk,khd->qhd", weights, value_seq, preferred_element_type=jnp.float32)
    return (output, highest + jnp.log(total))


def attend_backward(query_seq, key_seq, value_seq, grad_out, log_total, allowed):
    scores = jnp.einsum("qhd,khd->hqk", query_seq, key_seq, preferred_element_type=jnp.float32)
    if allowed is not None:
        scores = jnp.where(allowed[None], scores, NEGATIVE)
    probs = jnp.exp(scores - log_total)
    grad_probs = jnp.einsum("qhd,khd->hqk", grad_out, value_seq, preferred_element_type=jnp.float32)
    grad_scores = (probs * (grad_probs - jnp.sum(probs * grad_probs, -1, keepdims=True))).astype(
        jnp.bfloat16
    )
    grad_query = jnp.einsum(
        "hqk,khd->qhd", grad_scores, key_seq, preferred_element_type=jnp.float32
    ).astype(jnp.bfloat16)
    grad_key = jnp.einsum(
        "hqk,qhd->khd", grad_scores, query_seq, preferred_element_type=jnp.float32
    ).astype(jnp.bfloat16)
    grad_value = jnp.einsum(
        "hqk,qhd->khd", probs.astype(jnp.bfloat16), grad_out, preferred_element_type=jnp.float32
    ).astype(jnp.bfloat16)
    return (grad_query, grad_key, grad_value)


def local(
    inputs,
    encoder,
    lengths,
    self_qkv,
    self_out,
    cross_q,
    cross_kv,
    cross_out,
    fc_in,
    fc_out,
    norm_gain,
    norm_bias,
    proj_bias,
    fc_in_bias,
    cotangent,
):
    tp_count = lax.axis_size("tp")
    tp_place = lax.axis_index("tp")
    local_seqs, seq_len, width_all = inputs.shape
    group_seqs = local_seqs * tp_count
    group_rows = group_seqs * seq_len
    head_width = width_all // tp_count
    local_heads = head_width // HD
    ff_width = fc_in.shape[1]
    own_frames = encoder.shape[1]
    frames_all = own_frames * tp_count
    head_scale = HD ** (-0.5)
    w_qkv, w_self_out, w_cross_q, w_cross_kv, w_cross_out, w_fc_in, w_fc_out = (
        lax.all_gather(self_qkv, "fsdp", axis=1, tiled=True),
        lax.all_gather(self_out, "fsdp", axis=1, tiled=True),
        lax.all_gather(cross_q, "fsdp", axis=0, tiled=True),
        lax.all_gather(cross_kv, "fsdp", axis=1, tiled=True),
        lax.all_gather(cross_out, "fsdp", axis=1, tiled=True),
        lax.all_gather(fc_in, "fsdp", axis=0, tiled=True),
        lax.all_gather(fc_out, "fsdp", axis=1, tiled=True),
    )
    gains, shifts, biases, fc_bias_all = (
        lax.all_gather(norm_gain, ("fsdp", "tp"), axis=1, tiled=True),
        lax.all_gather(norm_bias, ("fsdp", "tp"), axis=1, tiled=True),
        lax.all_gather(proj_bias, ("fsdp", "tp"), axis=1, tiled=True),
        lax.all_gather(fc_in_bias, ("fsdp", "tp"), axis=0, tiled=True),
    )
    head_start = tp_place * head_width
    ff_start = tp_place * ff_width

    def column(vector):
        return lax.dynamic_slice_in_dim(vector, head_start, head_width)

    def placed(vector):
        return lax.dynamic_update_slice_in_dim(
            jnp.zeros((width_all,), jnp.float32), vector, head_start, 0
        )

    fc_bias = lax.dynamic_slice_in_dim(fc_bias_all, ff_start, ff_width)

    def gather_rows(normed):
        whole = lax.all_gather(normed.astype(jnp.bfloat16), "tp", axis=0, tiled=True)
        return whole.reshape(group_rows, width_all)

    def scatter_rows(partial_out):
        return lax.psum_scatter(
            partial_out.reshape(group_seqs, seq_len, width_all).astype(jnp.bfloat16),
            "tp",
            scatter_dimension=0,
            tiled=True,
        ).astype(jnp.float32)

    def gather_grads(grad_rows):
        whole = lax.all_gather(grad_rows, "tp", axis=0, tiled=True)
        return whole.reshape(group_rows, width_all)

    def scatter_grads(partial_grad):
        return lax.psum_scatter(
            partial_grad.reshape(group_seqs, seq_len, width_all).astype(jnp.bfloat16),
            "tp",
            scatter_dimension=0,
            tiled=True,
        ).astype(jnp.float32)

    def split_heads(flat):
        return flat.reshape(group_seqs, seq_len, local_heads, HD)

    positions = jnp.arange(seq_len)

    def self_mask(length):
        return (positions[None, :] <= positions[:, None]) & (positions[None, :] < length)

    inputs_f = inputs.astype(jnp.float32)
    normed_one, unit_one, inv_one = normalize(inputs_f, gains[0], shifts[0])
    rows_one = gather_rows(normed_one)
    query_one = ((matmul(rows_one, w_qkv[0]) + column(biases[0])) * head_scale).astype(jnp.bfloat16)
    key_one = matmul(rows_one, w_qkv[1]).astype(jnp.bfloat16)
    value_one = (matmul(rows_one, w_qkv[2]) + column(biases[1])).astype(jnp.bfloat16)

    def self_forward(item):
        return attend_forward(item[0], item[1], item[2], self_mask(item[3]))

    attended_one, total_one = lax.map(
        self_forward,
        (split_heads(query_one), split_heads(key_one), split_heads(value_one), lengths),
    )
    mixed_one = attended_one.astype(jnp.bfloat16).reshape(group_rows, head_width)
    first = inputs_f + scatter_rows(matmul(mixed_one, w_self_out)) + biases[2]
    normed_two, unit_two, inv_two = normalize(first, gains[1], shifts[1])
    rows_two = gather_rows(normed_two)
    query_two = ((matmul(rows_two, w_cross_q) + column(biases[3])) * head_scale).astype(
        jnp.bfloat16
    )
    head_shape = (group_seqs, frames_all, local_heads, HD)
    frames = lax.all_gather(encoder, "tp", axis=1, tiled=True)
    flat_frames = frames.reshape(group_seqs * frames_all, width_all)
    key_two = matmul(flat_frames, w_cross_kv[0]).astype(jnp.bfloat16).reshape(head_shape)
    value_two = (
        (matmul(flat_frames, w_cross_kv[1]) + column(biases[4]))
        .astype(jnp.bfloat16)
        .reshape(head_shape)
    )

    def cross_forward(item):
        return attend_forward(item[0], item[1], item[2], None)

    attended_two, total_two = lax.map(cross_forward, (split_heads(query_two), key_two, value_two))
    mixed_two = attended_two.astype(jnp.bfloat16).reshape(group_rows, head_width)
    second = first + scatter_rows(matmul(mixed_two, w_cross_out)) + biases[5]
    normed_three, unit_three, inv_three = normalize(second, gains[2], shifts[2])
    rows_three = gather_rows(normed_three)
    before = matmul(rows_three, w_fc_in) + fc_bias
    hidden = exact_gelu(before).astype(jnp.bfloat16)
    third = second + scatter_rows(matmul(hidden, w_fc_out)) + biases[6]
    result, unit_four, inv_four = normalize(third, gains[3], shifts[3])
    grad_result = cotangent.astype(jnp.float32)
    gain_four = row_sum(grad_result * unit_four)
    shift_four = row_sum(grad_result)
    grad_third = norm_back(grad_result, unit_four, inv_four, gains[3])
    branch_three = grad_third.astype(jnp.bfloat16)
    bias_six = row_sum(branch_three.astype(jnp.float32))
    down_three = gather_grads(branch_three)
    grad_hidden = against(down_three, w_fc_out)
    grad_fc_out = transposed(hidden, down_three)
    grad_before = jax.vjp(exact_gelu, before)[1](grad_hidden)[0].astype(jnp.bfloat16)
    grad_fc_bias = jnp.sum(grad_before.astype(jnp.float32), 0)
    grad_fc_in = transposed(rows_three, grad_before)
    grad_normed_three = scatter_grads(against(grad_before, w_fc_in))
    gain_three = row_sum(grad_normed_three * unit_three)
    shift_three = row_sum(grad_normed_three)
    grad_second = grad_third + norm_back(grad_normed_three, unit_three, inv_three, gains[2])
    branch_two = grad_second.astype(jnp.bfloat16)
    bias_five = row_sum(branch_two.astype(jnp.float32))
    down_two = gather_grads(branch_two)
    grad_mixed_two = against(down_two, w_cross_out).astype(jnp.bfloat16)
    grad_cross_out = transposed(mixed_two, down_two)

    def cross_backward(item):
        return attend_backward(item[0], item[1], item[2], item[3], item[4], None)

    grad_query_two, grad_key_two, grad_value_two = lax.map(
        cross_backward,
        (split_heads(query_two), key_two, value_two, split_heads(grad_mixed_two), total_two),
    )
    flat_query_two = grad_query_two.reshape(group_rows, head_width)
    flat_key_two = grad_key_two.reshape(group_seqs * frames_all, head_width)
    flat_value_two = grad_value_two.reshape(group_seqs * frames_all, head_width)
    grad_cross_q = transposed(rows_two, flat_query_two) * head_scale
    bias_three = jnp.sum(flat_query_two.astype(jnp.float32), 0) * head_scale
    bias_four = jnp.sum(flat_value_two.astype(jnp.float32), 0)
    grad_cross_kv = jnp.stack(
        [transposed(flat_frames, flat_key_two), transposed(flat_frames, flat_value_two)]
    )
    grad_frames = against(flat_key_two, w_cross_kv[0]) + against(flat_value_two, w_cross_kv[1])
    grad_encoder = lax.psum_scatter(
        grad_frames.reshape(group_seqs, frames_all, width_all).astype(jnp.bfloat16),
        "tp",
        scatter_dimension=1,
        tiled=True,
    ).astype(jnp.float32)
    grad_normed_two = scatter_grads(against(flat_query_two, w_cross_q) * head_scale)
    gain_two = row_sum(grad_normed_two * unit_two)
    shift_two = row_sum(grad_normed_two)
    grad_first = grad_second + norm_back(grad_normed_two, unit_two, inv_two, gains[1])
    branch_one = grad_first.astype(jnp.bfloat16)
    bias_two = row_sum(branch_one.astype(jnp.float32))
    down_one = gather_grads(branch_one)
    grad_mixed_one = against(down_one, w_self_out).astype(jnp.bfloat16)
    grad_self_out = transposed(mixed_one, down_one)

    def self_backward(item):
        return attend_backward(item[0], item[1], item[2], item[3], item[4], self_mask(item[5]))

    grad_query_one, grad_key_one, grad_value_one = lax.map(
        self_backward,
        (
            split_heads(query_one),
            split_heads(key_one),
            split_heads(value_one),
            split_heads(grad_mixed_one),
            total_one,
            lengths,
        ),
    )
    flat_query_one = grad_query_one.reshape(group_rows, head_width)
    flat_key_one = grad_key_one.reshape(group_rows, head_width)
    flat_value_one = grad_value_one.reshape(group_rows, head_width)
    grad_qkv = jnp.stack(
        [
            transposed(rows_one, flat_query_one) * head_scale,
            transposed(rows_one, flat_key_one),
            transposed(rows_one, flat_value_one),
        ]
    )
    bias_zero = jnp.sum(flat_query_one.astype(jnp.float32), 0) * head_scale
    bias_one = jnp.sum(flat_value_one.astype(jnp.float32), 0)
    grad_normed_one = scatter_grads(
        against(flat_query_one, w_qkv[0]) * head_scale
        + against(flat_key_one, w_qkv[1])
        + against(flat_value_one, w_qkv[2])
    )
    gain_one = row_sum(grad_normed_one * unit_one)
    shift_one = row_sum(grad_normed_one)
    grad_inputs = grad_first + norm_back(grad_normed_one, unit_one, inv_one, gains[0])
    grad_gains = jnp.stack([gain_one, gain_two, gain_three, gain_four])
    grad_shifts = jnp.stack([shift_one, shift_two, shift_three, shift_four])
    grad_biases = jnp.stack(
        [
            placed(bias_zero),
            placed(bias_one),
            bias_two,
            placed(bias_three),
            placed(bias_four),
            bias_five,
            bias_six,
        ]
    )
    grad_fc_bias_all = lax.dynamic_update_slice_in_dim(
        jnp.zeros((ff_width * tp_count,), jnp.float32), grad_fc_bias, ff_start, 0
    )
    small_gain, small_shift, small_bias, small_fc_bias = (
        lax.psum_scatter(grad_gains, ("fsdp", "tp"), scatter_dimension=1, tiled=True),
        lax.psum_scatter(grad_shifts, ("fsdp", "tp"), scatter_dimension=1, tiled=True),
        lax.psum_scatter(grad_biases, ("fsdp", "tp"), scatter_dimension=1, tiled=True),
        lax.psum_scatter(grad_fc_bias_all, ("fsdp", "tp"), scatter_dimension=0, tiled=True),
    )
    (
        owned_qkv,
        owned_self_out,
        owned_cross_q,
        owned_cross_kv,
        owned_cross_out,
        owned_fc_in,
        owned_fc_out,
    ) = (
        lax.psum_scatter(grad_qkv, "fsdp", scatter_dimension=1, tiled=True),
        lax.psum_scatter(grad_self_out, "fsdp", scatter_dimension=1, tiled=True),
        lax.psum_scatter(grad_cross_q, "fsdp", scatter_dimension=0, tiled=True),
        lax.psum_scatter(grad_cross_kv, "fsdp", scatter_dimension=1, tiled=True),
        lax.psum_scatter(grad_cross_out, "fsdp", scatter_dimension=1, tiled=True),
        lax.psum_scatter(grad_fc_in, "fsdp", scatter_dimension=0, tiled=True),
        lax.psum_scatter(grad_fc_out, "fsdp", scatter_dimension=1, tiled=True),
    )
    return (
        result.astype(jnp.bfloat16),
        grad_inputs,
        grad_encoder,
        owned_qkv,
        owned_self_out,
        owned_cross_q,
        owned_cross_kv,
        owned_cross_out,
        owned_fc_in,
        owned_fc_out,
        small_gain,
        small_shift,
        small_bias,
        small_fc_bias,
    )


def solution(mesh):
    return jax.shard_map(
        local,
        mesh=mesh,
        in_specs=(
            P(("fsdp", "tp"), None, None),
            P("fsdp", "tp", None),
            P("fsdp"),
            P(None, "fsdp", "tp"),
            P("tp", "fsdp"),
            P("fsdp", "tp"),
            P(None, "fsdp", "tp"),
            P("tp", "fsdp"),
            P("fsdp", "tp"),
            P("tp", "fsdp"),
            P(None, ("fsdp", "tp")),
            P(None, ("fsdp", "tp")),
            P(None, ("fsdp", "tp")),
            P(("fsdp", "tp")),
            P(("fsdp", "tp"), None, None),
        ),
        out_specs=(
            P(("fsdp", "tp"), None, None),
            P(("fsdp", "tp"), None, None),
            P("fsdp", "tp", None),
            P(None, "fsdp", "tp"),
            P("tp", "fsdp"),
            P("fsdp", "tp"),
            P(None, "fsdp", "tp"),
            P("tp", "fsdp"),
            P("fsdp", "tp"),
            P("tp", "fsdp"),
            P(None, ("fsdp", "tp")),
            P(None, ("fsdp", "tp")),
            P(None, ("fsdp", "tp")),
            P(("fsdp", "tp")),
        ),
        check_vma=False,
    )
```

profile of v0, /device:TPU:0, one launch (start us, length us, event | category | flops | bytes accessed | tf_op | source)
XLA Modules:
  0.0 1686.6 jit_solution(319161292977433544)
XLA Ops:
  10.9 70.4 %all-gather = f32[32,24,4]{1,2,0:T(4,128)S(1)} all-gather(f32[1,24,4]{1,2,0:T(4,128)} %bitcast.408), channel_id=1, replica_groups=mesh['fsdp'=8,'tp'=4] {'fsdp','tp'}, dimensions={0}, use_global_device_ids=true | all-gather | bytes 12672 | tf_op jit(solution)/shard_map/all_gather | solution.py:122
  82.0 64.1 %all-gather.1 = f32[32,24,4]{1,2,0:T(4,128)S(1)} all-gather(f32[1,24,4]{1,2,0:T(4,128)} %bitcast.409), channel_id=1, replica_groups=mesh['fsdp'=8,'tp'=4] {'fsdp','tp'}, dimensions={0}, use_global_device_ids=true | all-gather | bytes 12672 | tf_op jit(solution)/shard_map/all_gather | solution.py:123
  149.3 69.4 %all-gather.2 = f32[32,24,7]{1,2,0:T(8,128)S(1)} all-gather(f32[1,24,7]{1,2,0:T(8,128)S(1)} %bitcast.407), channel_id=1, replica_groups=mesh['fsdp'=8,'tp'=4] {'fsdp','tp'}, dimensions={0}, use_global_device_ids=true | all-gather | bytes 22176 | tf_op jit(solution)/shard_map/all_gather | solution.py:124
  218.9 9.0 all_gather.59
  229.2 11.9 all_gather.57
  254.8 19.2 %while.58 = (s32[]{:T(128)}, bf16[4,448,3,64]{1,3,2,0:T(8,128)(2,1)S(1)}, f32[4,3,448,1]{2,1,3,0:T(4,128)}, bf16[4,448,3,64]{1,3,2,0:T(8,128)(2,1)S(1)}, s32[4]{...) while((s32[]{:T(128)}, ...), condition=%wide.region_5.6_spmd.clone.clone, body=%wide.region_2.5_spmd.clone.clone.sunk | while | flops 159960192 | bytes 9467121 | solution.py:182
  277.5 51.6 %reduce-scatter.27.cloned.1.call-done = bf16[1,448,768]{2,1,0:T(8,128)(2,1)} async-done(((bf16[4,448,768]{2,1,0:T(8,128)(2,1)}), bf16[1,448,768]{2,1,0:T(8,128)(2,1)}) %reduce-scatter.27.cloned.1.call-update) | async-done | bytes 688144 | tf_op jit(solution)/shard_map/reduce_scatter | solution.py:145
  334.3 9.5 all_gather.64
  343.8 9.7 all_gather.63
  355.0 10.8 all_gather.61
  365.8 24.4 %all-gather.17.cloned.1.call-done = bf16[4,448,768]{2,1,0:T(8,128)(2,1)} async-done(((bf16[1,448,768]{2,1,0:T(8,128)(2,1)}), bf16[4,448,768]{2,1,0:T(8,128)(2,1)}) %all-gather.17.cloned.1.call-update) | async-done | bytes 2752528 | tf_op jit(solution)/shard_map/all_gather | solution.py:141
  395.0 158.6 %all-gather.15.cloned.1.call-done = bf16[4,1500,768]{2,0,1:T(4,128)(2,1)} async-done(((bf16[4,375,768]{2,0,1:T(4,128)(2,1)}), bf16[4,1500,768]{2,0,1:T(4,128)(2,1)}) %all-gather.15.cloned.1.call-update) | async-done | bytes 9216016 | tf_op jit(solution)/shard_map/all_gather | solution.py:194
  561.9 10.7 reshape.514
  600.6 29.4 %while.56 = (s32[]{:T(128)}, bf16[4,448,3,64]{1,3,2,0:T(8,128)(2,1)}, f32[4,3,448,1]{2,1,3,0:T(4,128)S(1)}, bf16[4,1500,3,64]{1,3,2,0:T(8,128)(2,1)}, bf16[4,448...) while((s32[]{:T(128)}, bf16[4,448,3,64]{1,3,2,0:T(8,128)(2,1)}, ...), condition=%wide.region_12.13_spmd, body=%wide.region_9.12_spmd.sunk | while | flops 528190656 | bytes 31719312 | solution.py:206
  634.2 52.0 %reduce-scatter.29.cloned.1.call-done = bf16[1,448,768]{2,1,0:T(8,128)(2,1)} async-done(((bf16[4,448,768]{2,1,0:T(8,128)(2,1)}), bf16[1,448,768]{2,1,0:T(8,128)(2,1)}) %reduce-scatter.29.cloned.1.call-update) | async-done | bytes 688144 | tf_op jit(solution)/shard_map/reduce_scatter | solution.py:145
  691.2 43.9 %all-reduce = f32[3072]{0:T(1024)S(1)} all-reduce(f32[3072]{0:T(1024)S(1)} %dynamic-update-slice), channel_id=1, replica_groups=mesh['fsdp'=8,'tp'=4] {'fsdp','tp'}, use_global_device_ids=true, to_apply=%add | all-reduce | flops 3072 | bytes 24576
  735.1 12.6 all-gather.19.cloned.1.call-done
  747.7 17.3 %multiply_convert_fusion.3 = (bf16[1792,768]{1,0:T(8,128)(2,1)}, f32[1792,768]{1,0:T(8,128)}, f32[1792,768]{1,0:T(8,128)}) fusion(f32[768]{0:T(1024)S(1)} %dynamic_slice.77, bf16[1792,768]{1,0:T(8,128)(2,1)} %bitcast.416, bf16[768,768]{1,0:T(8,128)(2,1)} %all-gather.21.cloned.1.call-done), kind=kOutput, calls=%fused_computation.124 | convolution fusion | flops 2204762112 | bytes 17697792 | tf_op jit(solution)/shard_map/dot_general | solution.py:28
  778.1 54.3 %reduce-scatter.31.cloned.1.call-done = bf16[1,448,768]{2,1,0:T(8,128)(2,1)} async-done(((bf16[4,448,768]{2,1,0:T(8,128)(2,1)}), bf16[1,448,768]{2,1,0:T(8,128)(2,1)}) %reduce-scatter.31.cloned.1.call-update) | async-done | bytes 688144 | tf_op jit(solution)/shard_map/reduce_scatter | solution.py:145
  838.0 56.2 %all-gather.25.cloned.1.call-done = bf16[4,448,768]{2,1,0:T(8,128)(2,1)} async-done(((bf16[1,448,768]{2,1,0:T(8,128)(2,1)}), bf16[4,448,768]{2,1,0:T(8,128)(2,1)}) %all-gather.25.cloned.1.call-update) | async-done | bytes 2752528 | tf_op jit(solution)/shard_map/all_gather | solution.py:153
  894.2 10.0 convert_reduce_fusion
  908.3 53.0 %reduce-scatter.33.cloned.1.call-done = bf16[1,448,768]{2,1,0:T(8,128)(2,1)} async-done(((bf16[4,448,768]{2,1,0:T(8,128)(2,1)}), bf16[1,448,768]{2,1,0:T(8,128)(2,1)}) %reduce-scatter.33.cloned.1.call-update) | async-done | bytes 688144 | tf_op jit(solution)/shard_map/reduce_scatter | solution.py:157
  968.7 56.2 %all-gather.27.cloned.1.call-done = bf16[4,448,768]{2,1,0:T(8,128)(2,1)} async-done(((bf16[1,448,768]{2,1,0:T(8,128)(2,1)}), bf16[4,448,768]{2,1,0:T(8,128)(2,1)}) %all-gather.27.cloned.1.call-update) | async-done | bytes 2752528 | tf_op jit(solution)/shard_map/all_gather | solution.py:153
  1035.1 48.7 %while.57 = (s32[]{:T(128)}, bf16[4,448,3,64]{1,3,2,0:T(8,128)(2,1)}, bf16[4,1500,3,64]{1,3,2,0:T(8,128)(2,1)}, bf16[4,1500,3,64]{1,3,2,0:T(8,128)(2,1)}, bf16[4...) while((s32[]{:T(128)}, ...), condition=%wide.region_26.27_spmd, body=%wide.region_24.26_spmd.sunk | while | flops 1309044736 | bytes 67793800 | solution.py:240
  1090.1 52.8 %reduce-scatter.35.cloned.1.call-done = bf16[1,448,768]{2,1,0:T(8,128)(2,1)} async-done(((bf16[4,448,768]{2,1,0:T(8,128)(2,1)}), bf16[1,448,768]{2,1,0:T(8,128)(2,1)}) %reduce-scatter.35.cloned.1.call-update) | async-done | bytes 688144 | tf_op jit(solution)/shard_map/reduce_scatter | solution.py:157
  1199.9 10.1 fusion.163
  1210.0 13.0 add_convert_fusion
  1223.0 10.6 convert_element_type.240
  1233.6 36.9 %copy.119 = bf16[4,1500,768]{2,0,1:T(4,128)(2,1)} copy(bf16[4,1500,768]{2,1,0:T(8,128)(2,1)} %convert_element_type.240) | data formatting | bytes 18432000 | tf_op jit(solution)/shard_map/convert_element_type | solution.py:255
  1280.4 35.1 %while.59 = (s32[]{:T(128)}, bf16[4,448,3,64]{1,3,2,0:T(8,128)(2,1)}, bf16[4,448,3,64]{1,3,2,0:T(8,128)(2,1)}, bf16[4,448,3,64]{1,3,2,0:T(8,128)(2,1)}, bf16[4,4...) while((s32[]{:T(128)}, ...), condition=%wide.region_32.33_spmd.clone.clone, body=%wide.region_30.32_spmd.clone.clone.sunk | while | flops 390827136 | bytes 21527560 | solution.py:273
  1372.7 249.1 %all-reduce.9.cloned.1.call-done = bf16[4,1500,768]{2,0,1:T(4,128)(2,1)} async-done(((bf16[4,1500,768]{2,0,1:T(4,128)(2,1)}), bf16[4,1500,768]{2,0,1:T(4,128)(2,1)}) %all-reduce.9.cloned.1.call-update) | async-done | bytes 9216016
  1632.6 40.6 %all-reduce.6 = (f32[4,768]{1,0:T(4,128)S(1)}, f32[4,768]{1,0:T(4,128)S(1)}, f32[7,768]{1,0:T(8,128)S(1)}, f32[3072]{0:T(1024)S(1)}) all-reduce(f32[4,768]{1,0:T(4,128)S(1)} %pad_maximum_fusion.2, f32[4,768]{1,0:T(4,128)S(1)} %pad_maximum_fusion.3, f32[7,768]{1,0:T(8,128)S(1)} %stack.96, ...), channel_id=16, replica_groups=mesh['fsdp'=8,'tp'=4] {'fsdp','tp'}, use_global_device_ids=true, to_apply=%region_48.49.clone | all-reduce | flops 14592 | bytes 116736
  (530 shorter events, 399.0 us)
Async XLA Ops:
  8.0 141.2 %copy-start.61 = (bf16[192,96]{1,0:T(8,128)(2,1)S(1)}, bf16[192,96]{1,0:T(8,128)(2,1)}, u32[]{:S(2)}) copy-start(bf16[192,96]{1,0:T(8,128)(2,1)} %param.27) | copy-start | bytes 110596
  8.0 141.3 %copy-start.77 = (f32[7,24]{1,0:T(8,128)S(1)}, f32[7,24]{1,0:T(8,128)}, u32[]{:S(2)}) copy-start(f32[7,24]{1,0:T(8,128)} %param.35) | copy-start | bytes 2020
  8.0 221.2 %copy-start.49 = (bf16[3,96,192]{2,1,0:T(8,128)(2,1)S(1)}, bf16[3,96,192]{2,1,0:T(8,128)(2,1)}, u32[]{:S(2)}) copy-start(bf16[3,96,192]{2,1,0:T(8,128)(2,1)} %param.26) | copy-start | bytes 331780
  8.0 233.0 %all-gather.13.cloned.1.call-start = ((), (), s32[]{:S(2)}) async-start(), calls=%async_computation.13 | async-start | bytes 3440640 | tf_op jit(solution)/shard_map/all_gather | solution.py:141
  9.4 139.9 %copy-start.56 = (f32[448]{0:T(512)}, f32[448]{0:T(512)S(1)}, u32[]{:S(2)}) copy-start(f32[448]{0:T(512)S(1)} %broadcast_multiply_fusion.13) | copy-start | bytes 5380
  10.9 138.4 %copy-start.63 = (f32[448]{0:T(512)}, f32[448]{0:T(512)S(1)}, u32[]{:S(2)}) copy-start(f32[448]{0:T(512)S(1)} %add_rsqrt_fusion.3) | copy-start | bytes 5380
  82.0 250.2 %copy-start.53 = (f32[768]{0:T(1024)}, f32[768]{0:T(1024)S(1)}, u32[]{:S(2)}) copy-start(f32[768]{0:T(1024)S(1)} %get-tuple-element.457) | copy-start | bytes 9220
  149.1 180.1 %reduce-scatter.27.cloned.1.call-start = ((), (), s32[]{:S(2)}) async-start(), calls=%async_computation.14 | async-start | bytes 3440640 | tf_op jit(solution)/shard_map/reduce_scatter | solution.py:145
  229.1 457.1 %copy-start.47 = (f32[768]{0:T(1024)}, f32[768]{0:T(1024)S(1)}, u32[]{:S(2)}) copy-start(f32[768]{0:T(1024)S(1)} %get-tuple-element.558) | copy-start | bytes 9220
  277.5 112.8 %all-gather.17.cloned.1.call-start = ((), (), s32[]{:S(2)}) async-start(), calls=%async_computation.16 | async-start | bytes 3440640 | tf_op jit(solution)/shard_map/all_gather | solution.py:141
  333.5 220.0 %all-gather.15.cloned.1.call-start = ((), (), s32[]{:S(2)}) async-start(), calls=%async_computation.15 | async-start | bytes 11520000 | tf_op jit(solution)/shard_map/all_gather | solution.py:194
  334.1 352.1 %reduce-scatter.29.cloned.1.call-start = ((), (), s32[]{:S(2)}) async-start(), calls=%async_computation.17 | async-start | bytes 3440640 | tf_op jit(solution)/shard_map/reduce_scatter | solution.py:145
  633.6 101.5 %all-gather.21.cloned.1.call-start = ((), (), s32[]{:S(2)}) async-start(), calls=%async_computation.19 | async-start | bytes 1327104 | tf_op jit(solution)/shard_map/all_gather | solution.py:118
  634.2 113.5 %all-gather.19.cloned.1.call-start = ((), (), s32[]{:S(2)}) async-start(), calls=%async_computation.18 | async-start | bytes 3440640 | tf_op jit(solution)/shard_map/all_gather | solution.py:141
  690.2 81.8 %all-gather.23.cloned.1.call-start = ((), (), s32[]{:S(2)}) async-start(), calls=%async_computation.20 | async-start | bytes 1327104 | tf_op jit(solution)/shard_map/all_gather | solution.py:119
  690.8 141.7 %reduce-scatter.31.cloned.1.call-start = ((), (), s32[]{:S(2)}) async-start(), calls=%async_computation.21 | async-start | bytes 3440640 | tf_op jit(solution)/shard_map/reduce_scatter | solution.py:145
  778.1 116.2 %all-gather.25.cloned.1.call-start = ((), (), s32[]{:S(2)}) async-start(), calls=%async_computation.22 | async-start | bytes 3440640 | tf_op jit(solution)/shard_map/all_gather | solution.py:153
  837.8 123.6 %reduce-scatter.33.cloned.1.call-start = ((), (), s32[]{:S(2)}) async-start(), calls=%async_computation.23 | async-start | bytes 3440640 | tf_op jit(solution)/shard_map/reduce_scatter | solution.py:157
  908.2 116.6 %all-gather.27.cloned.1.call-start = ((), (), s32[]{:S(2)}) async-start(), calls=%async_computation.24 | async-start | bytes 3440640 | tf_op jit(solution)/shard_map/all_gather | solution.py:153
  968.4 174.5 %reduce-scatter.35.cloned.1.call-start = ((), (), s32[]{:S(2)}) async-start(), calls=%async_computation.25 | async-start | bytes 3440640 | tf_op jit(solution)/shard_map/reduce_scatter | solution.py:157
  1089.8 181.1 %all-gather.29.cloned.1.call-start = ((), (), s32[]{:S(2)}) async-start(), calls=%async_computation.26 | async-start | bytes 3440640 | tf_op jit(solution)/shard_map/all_gather | solution.py:153
  1148.0 221.2 %reduce-scatter.51.cloned.1.call-start = ((), (), s32[]{:S(2)}) async-start(), calls=%async_computation.34 | async-start | bytes 884736
  1171.5 199.3 %reduce-scatter.49.cloned.1.call-start = ((), (), s32[]{:S(2)}) async-start(), calls=%async_computation.33 | async-start | bytes 1327104
  1199.7 422.1 %all-reduce.9.cloned.1.call-start = ((), (), s32[]{:S(2)}) async-start(), calls=%async_computation.35 | async-start | bytes 18432000
  1270.6 356.5 %reduce-scatter.45.cloned.1.call-start = ((), (), s32[]{:S(2)}) async-start(), calls=%async_computation.31 | async-start | bytes 884736
  1322.3 306.5 %reduce-scatter.43.cloned.1.call-start = ((), (), s32[]{:S(2)}) async-start(), calls=%async_computation.30 | async-start | bytes 2211840
  1342.7 287.9 %reduce-scatter.37.cloned.1.call-start = ((), (), s32[]{:S(2)}) async-start(), calls=%async_computation.27 | async-start | bytes 3440640 | tf_op jit(solution)/shard_map/reduce_scatter | solution.py:157
  1347.5 331.4 %reduce-scatter.39.cloned.1.call-start = ((), (), s32[]{:S(2)}) async-start(), calls=%async_computation.28 | async-start | bytes 2654208 | tf_op jit(solution)/shard_map/reduce_scatter | solution.py:340
  1354.3 324.5 %reduce-scatter.41.cloned.1.call-start = ((), (), s32[]{:S(2)}) async-start(), calls=%async_computation.29 | async-start | bytes 2654208 | tf_op jit(solution)/shard_map/reduce_scatter | solution.py:341
  1361.2 317.7 %reduce-scatter.47.cloned.1.call-start = ((), (), s32[]{:S(2)}) async-start(), calls=%async_computation.32 | async-start | bytes 884736
  1372.6 253.5 %copy-start.18 = (bf16[4,448,3,64]{1,3,2,0:T(8,128)(2,1)S(1)}, bf16[4,448,3,64]{1,3,2,0:T(8,128)(2,1)}, u32[]{:S(2)}) copy-start(bf16[4,448,3,64]{1,3,2,0:T(8,128)(2,1)} %get-tuple-element.211) | copy-start | bytes 2064388
  1372.7 253.7 %copy-start.20 = (bf16[4,448,3,64]{1,3,2,0:T(8,128)(2,1)S(1)}, bf16[4,448,3,64]{1,3,2,0:T(8,128)(2,1)}, u32[]{:S(2)}) copy-start(bf16[4,448,3,64]{1,3,2,0:T(8,128)(2,1)} %get-tuple-element.209) | copy-start | bytes 2064388
  (84 other events, 1240.3 us)
Sparse Core Ops, SparseCore 0:
  149.2 56.4 all-gather.12
  277.6 51.5 reduce-scatter.26
  333.7 56.5 all-gather.16
  391.7 161.8 all-gather.14
  633.7 52.4 reduce-scatter.28
  1270.7 351.0 all-reduce.8
Sparse Core Ops, SparseCore 1:
  636.0 22.0 all-gather.20
  690.3 57.4 all-gather.18
  749.5 22.5 all-gather.22
  778.1 54.3 reduce-scatter.30
  837.9 56.3 all-gather.24
  908.3 53.0 reduce-scatter.32
  968.5 56.4 all-gather.26
  1089.9 53.0 reduce-scatter.34
  1148.1 56.4 all-gather.28
  1207.7 33.6 reduce-scatter.50
  1244.4 36.6 reduce-scatter.48
  1322.4 34.5 reduce-scatter.44
  1360.2 40.0 reduce-scatter.42
  1402.6 120.2 reduce-scatter.36
  1526.8 42.2 reduce-scatter.38
  1573.0 42.2 reduce-scatter.40
  1619.0 35.1 reduce-scatter.46
where the time goes:
time: 1690 us
  waiting for transfers between devices  830 us (49%)
  blocking collectives  339 us (20%)
  matrix products  238 us (14%)
  local copies, waits for them, and re-layouts  189 us (11%)
  other arithmetic  68.7 us (4%)
  between operations  18.1 us (1%)
    unnamed x29, waiting for transfers between devices  251 us
    all_gather x1, waiting for transfers between devices, local(): frames = lax.all_gather(encoder, 'tp', axis=1, tiled=True)  159 us
    reduce_scatter x3, waiting for transfers between devices, scatter_rows(): lax.psum_scatter(partial_out.reshape(group_seqs, seq_len, width_all).asty...  158 us
    all_gather x3, waiting for transfers between devices, gather_grads(): whole = lax.all_gather(grad_rows, 'tp', axis=0, tiled=True)  112 us
    reduce_scatter x3, waiting for transfers between devices, scatter_grads(): lax.psum_scatter(partial_grad.reshape(group_seqs, seq_len, width_all).ast...  106 us
    unnamed x2, blocking collectives  84.5 us
    all_gather x1, blocking collectives, local(): lax.all_gather(norm_gain, ('fsdp', 'tp'), axis=1, tiled=True)  70.4 us
    all_gather x1, blocking collectives, local(): lax.all_gather(proj_bias, ('fsdp', 'tp'), axis=1, tiled=True)  69.4 us
  transfers between devices with their start and end apart: 23, of which 12 were waited for; matrix products, arithmetic and copies ran while one was open for 16% of the time, Pallas kernels for 0%

commit v1 on v0

--- a/solution.py
+++ b/solution.py
@@ -191,7 +191,23 @@
         jnp.bfloat16
     )
     head_shape = (group_seqs, frames_all, local_heads, HD)
-    frames = lax.all_gather(encoder, "tp", axis=1, tiled=True)
+    n_axis = lax.psum(1, axis_name="tp")
+    pages = []
+    for q in range(n_axis):
+        pages.append((q, (q + 1) % n_axis))
+    by_rank = []
+    for q in range(n_axis):
+        by_rank.append((q, (q - 1) % n_axis))
+    outer, kept_arr = ([encoder], [encoder])
+    for _ in range(n_axis // 2):
+        res = lax.ppermute(outer[-1], axis_name="tp", perm=pages)
+        outer.append(res)
+    for _ in range((n_axis - 1) // 2):
+        arr_out = lax.ppermute(kept_arr[-1], perm=by_rank, axis_name="tp")
+        kept_arr.append(arr_out)
+    piece_out = jnp.concatenate([*outer[::-1], *kept_arr[1:]], axis=1)
+    top = lax.axis_index("tp")
+    frames = jnp.roll(piece_out, shift=(top - n_axis // 2) * encoder.shape[1], axis=1)
     flat_frames = frames.reshape(group_seqs * frames_all, width_all)
     key_two = matmul(flat_frames, w_cross_kv[0]).astype(jnp.bfloat16).reshape(head_shape)
     value_two = (

time: 1690 us -> 1690 us (level)
  waiting for transfers between devices: 830 us -> 794 us
  local copies, waits for them, and re-layouts: 189 us -> 210 us
    ppermute x0 -> x3, waiting for transfers between devices: none -> 199 us  [the longest x2 150 us: local(): res = lax.ppermute(outer[-1], axis_name='tp', perm=pages)]
    all_gather x1 -> x0, waiting for transfers between devices: 159 us -> none  [local(): frames = lax.all_gather(encoder, 'tp', axis=1, tiled=True)]
    reduce_scatter x3, waiting for transfers between devices: 158 us -> 107 us  [scatter_rows(): lax.psum_scatter(partial_out.reshape(group_seqs, seq_len, width_all).asty...]
    all_gather x3, waiting for transfers between devices: 37 us -> 12.7 us  [gather_rows(): lax.all_gather(normed.astype(jnp.bfloat16), 'tp', axis=0, tiled=True)]
    unnamed x190 -> x197, local copies, waits for them, and re-layouts: 32.3 us -> 44.5 us
    unnamed x29 -> x28, waiting for transfers between devices: 251 us -> 250 us
  transfers between devices with their start and end apart: 23 -> 25, of which waited for: 12 -> 12; matrix products, arithmetic and copies ran while one was open for 16% -> 20% of each run, Pallas kernels for 0% -> 0%
where the time goes in v1:
time: 1690 us; the launch traced here: 1680 us
  waiting for transfers between devices  794 us (47%)
  blocking collectives  340 us (20%)
  matrix products  243 us (14%)
  local copies, waits for them, and re-layouts  210 us (12%)
  other arithmetic  68.7 us (4%)
  between operations  18.2 us (1%)
    unnamed x28, waiting for transfers between devices  250 us
    ppermute x2, waiting for transfers between devices, local(): res = lax.ppermute(outer[-1], axis_name='tp', perm=pages)  150 us
    all_gather x3, waiting for transfers between devices, gather_grads(): whole = lax.all_gather(grad_rows, 'tp', axis=0, tiled=True)  112 us
    reduce_scatter x3, waiting for transfers between devices, scatter_rows(): lax.psum_scatter(partial_out.reshape(group_seqs, seq_len, width_all).asty...  107 us
    reduce_scatter x3, waiting for transfers between devices, scatter_grads(): lax.psum_scatter(partial_grad.reshape(group_seqs, seq_len, width_all).ast...  106 us
    unnamed x2, blocking collectives  84.5 us
    all_gather x1, blocking collectives, local(): lax.all_gather(norm_gain, ('fsdp', 'tp'), axis=1, tiled=True)  70.4 us
    all_gather x1, blocking collectives, local(): lax.all_gather(proj_bias, ('fsdp', 'tp'), axis=1, tiled=True)  69.4 us
  transfers between devices with their start and end apart: 25, of which 12 were waited for; matrix products, arithmetic and copies ran while one was open for 20% of the time, Pallas kernels for 0%

profile of v1, /device:TPU:0, one launch (start us, length us, event | category | flops | bytes accessed | tf_op | source)
XLA Modules:
  0.0 1681.2 jit_solution(12278374822525854724)
XLA Ops:
  10.9 70.4 %all-gather = f32[32,24,4]{1,2,0:T(4,128)S(1)} all-gather(f32[1,24,4]{1,2,0:T(4,128)} %bitcast.404), channel_id=1, replica_groups=mesh['fsdp'=8,'tp'=4] {'fsdp','tp'}, dimensions={0}, use_global_device_ids=true | all-gather | bytes 12672 | tf_op jit(solution)/shard_map/all_gather | solution.py:122
  82.0 64.1 %all-gather.1 = f32[32,24,4]{1,2,0:T(4,128)S(1)} all-gather(f32[1,24,4]{1,2,0:T(4,128)} %bitcast.405), channel_id=1, replica_groups=mesh['fsdp'=8,'tp'=4] {'fsdp','tp'}, dimensions={0}, use_global_device_ids=true | all-gather | bytes 12672 | tf_op jit(solution)/shard_map/all_gather | solution.py:123
  149.3 69.4 %all-gather.2 = f32[32,24,7]{1,2,0:T(8,128)S(1)} all-gather(f32[1,24,7]{1,2,0:T(8,128)S(1)} %bitcast.403), channel_id=1, replica_groups=mesh['fsdp'=8,'tp'=4] {'fsdp','tp'}, dimensions={0}, use_global_device_ids=true | all-gather | bytes 22176 | tf_op jit(solution)/shard_map/all_gather | solution.py:124
  218.9 9.0 all_gather.56
  229.2 11.9 all_gather.54
  254.8 19.2 %while.58 = (s32[]{:T(128)}, bf16[4,448,3,64]{1,3,2,0:T(8,128)(2,1)S(1)}, f32[4,3,448,1]{2,1,3,0:T(4,128)}, bf16[4,448,3,64]{1,3,2,0:T(8,128)(2,1)S(1)}, s32[4]{...) while((s32[]{:T(128)}, ...), condition=%wide.region_5.6_spmd.clone.clone, body=%wide.region_2.5_spmd.clone.clone.sunk | while | flops 159960192 | bytes 9467121 | solution.py:182
  278.2 98.0 %collective-permute-done = bf16[4,375,768]{2,0,1:T(4,128)(2,1)S(1)} collective-permute-done((bf16[4,375,768]{2,0,1:T(4,128)(2,1)}, bf16[4,375,768]{2,0,1:T(4,128)(2,1)S(1)}, u32[]{:S(2)}, u32[]{:S(2)}) %collective-permute-start) | collective-permute-done | bytes 2304032 | tf_op jit(solution)/shard_map/ppermute | solution.py:203
  384.6 9.2 all_gather.60
  393.8 10.4 all_gather.59
  405.0 10.9 all_gather.57
  416.0 51.8 %collective-permute-done.1 = bf16[4,375,768]{2,0,1:T(4,128)(2,1)} collective-permute-done((bf16[4,375,768]{2,0,1:T(4,128)(2,1)S(1)}, bf16[4,375,768]{2,0,1:T(4,128)(2,1)}, u32[]{:S(2)}, u32[]{:S(2)}) %collective-permute-start.1) | collective-permute-done | bytes 2304032 | tf_op jit(solution)/shard_map/ppermute | solution.py:203
  472.9 48.7 %collective-permute-done.2 = bf16[4,375,768]{2,0,1:T(4,128)(2,1)} collective-permute-done((bf16[4,375,768]{2,0,1:T(4,128)(2,1)}, bf16[4,375,768]{2,0,1:T(4,128)(2,1)}, u32[]{:S(2)}, u32[]{:S(2)}) %collective-permute-start.2) | collective-permute-done | bytes 2304032 | tf_op jit(solution)/shard_map/ppermute | solution.py:206
  545.2 10.8 reshape.514
  594.5 29.1 %while.56 = (s32[]{:T(128)}, bf16[4,448,3,64]{1,3,2,0:T(8,128)(2,1)}, f32[4,3,448,1]{2,1,3,0:T(4,128)S(1)}, bf16[4,1500,3,64]{1,3,2,0:T(8,128)(2,1)}, bf16[4,448...) while((s32[]{:T(128)}, bf16[4,448,3,64]{1,3,2,0:T(8,128)(2,1)}, ...), condition=%wide.region_12.13_spmd, body=%wide.region_9.12_spmd.sunk | while | flops 528190656 | bytes 31719312 | solution.py:222
  627.9 52.6 %reduce-scatter.29.cloned.1.call-done = bf16[1,448,768]{2,1,0:T(8,128)(2,1)} async-done(((bf16[4,448,768]{2,1,0:T(8,128)(2,1)}), bf16[1,448,768]{2,1,0:T(8,128)(2,1)}) %reduce-scatter.29.cloned.1.call-update) | async-done | bytes 688144 | tf_op jit(solution)/shard_map/reduce_scatter | solution.py:145
  685.5 43.9 %all-reduce = f32[3072]{0:T(1024)S(1)} all-reduce(f32[3072]{0:T(1024)S(1)} %dynamic-update-slice), channel_id=1, replica_groups=mesh['fsdp'=8,'tp'=4] {'fsdp','tp'}, use_global_device_ids=true, to_apply=%add | all-reduce | flops 3072 | bytes 24576
  729.5 12.7 all-gather.16.cloned.1.call-done
  742.1 17.3 %multiply_convert_fusion.3 = (bf16[1792,768]{1,0:T(8,128)(2,1)}, f32[1792,768]{1,0:T(8,128)}, f32[1792,768]{1,0:T(8,128)}) fusion(f32[768]{0:T(1024)S(1)} %dynamic_slice.82, bf16[1792,768]{1,0:T(8,128)(2,1)} %bitcast.412, bf16[768,768]{1,0:T(8,128)(2,1)} %all-gather.18.cloned.1.call-done), kind=kOutput, calls=%fused_computation.124 | convolution fusion | flops 2204762112 | bytes 17697792 | tf_op jit(solution)/shard_map/dot_general | solution.py:28
  772.5 54.3 %reduce-scatter.31.cloned.1.call-done = bf16[1,448,768]{2,1,0:T(8,128)(2,1)} async-done(((bf16[4,448,768]{2,1,0:T(8,128)(2,1)}), bf16[1,448,768]{2,1,0:T(8,128)(2,1)}) %reduce-scatter.31.cloned.1.call-update) | async-done | bytes 688144 | tf_op jit(solution)/shard_map/reduce_scatter | solution.py:145
  832.4 56.2 %all-gather.22.cloned.1.call-done = bf16[4,448,768]{2,1,0:T(8,128)(2,1)} async-done(((bf16[1,448,768]{2,1,0:T(8,128)(2,1)}), bf16[4,448,768]{2,1,0:T(8,128)(2,1)}) %all-gather.22.cloned.1.call-update) | async-done | bytes 2752528 | tf_op jit(solution)/shard_map/all_gather | solution.py:153
  888.6 10.0 convert_reduce_fusion
  902.6 53.1 %reduce-scatter.33.cloned.1.call-done = bf16[1,448,768]{2,1,0:T(8,128)(2,1)} async-done(((bf16[4,448,768]{2,1,0:T(8,128)(2,1)}), bf16[1,448,768]{2,1,0:T(8,128)(2,1)}) %reduce-scatter.33.cloned.1.call-update) | async-done | bytes 688144 | tf_op jit(solution)/shard_map/reduce_scatter | solution.py:157
  963.2 56.2 %all-gather.24.cloned.1.call-done = bf16[4,448,768]{2,1,0:T(8,128)(2,1)} async-done(((bf16[1,448,768]{2,1,0:T(8,128)(2,1)}), bf16[4,448,768]{2,1,0:T(8,128)(2,1)}) %all-gather.24.cloned.1.call-update) | async-done | bytes 2752528 | tf_op jit(solution)/shard_map/all_gather | solution.py:153
  1029.7 48.7 %while.57 = (s32[]{:T(128)}, bf16[4,448,3,64]{1,3,2,0:T(8,128)(2,1)}, bf16[4,1500,3,64]{1,3,2,0:T(8,128)(2,1)}, bf16[4,1500,3,64]{1,3,2,0:T(8,128)(2,1)}, bf16[4...) while((s32[]{:T(128)}, ...), condition=%wide.region_26.27_spmd, body=%wide.region_24.26_spmd.sunk | while | flops 1309044736 | bytes 67793800 | solution.py:256
  1084.6 53.0 %reduce-scatter.35.cloned.1.call-done = bf16[1,448,768]{2,1,0:T(8,128)(2,1)} async-done(((bf16[4,448,768]{2,1,0:T(8,128)(2,1)}), bf16[1,448,768]{2,1,0:T(8,128)(2,1)}) %reduce-scatter.35.cloned.1.call-update) | async-done | bytes 688144 | tf_op jit(solution)/shard_map/reduce_scatter | solution.py:157
  1194.4 10.1 fusion.163
  1204.5 13.0 add_convert_fusion
  1217.5 10.6 convert_element_type.240
  1228.1 36.9 %copy.119 = bf16[4,1500,768]{2,0,1:T(4,128)(2,1)} copy(bf16[4,1500,768]{2,1,0:T(8,128)(2,1)} %convert_element_type.240) | data formatting | bytes 18432000 | tf_op jit(solution)/shard_map/convert_element_type | solution.py:271
  1274.8 35.1 %while.59 = (s32[]{:T(128)}, bf16[4,448,3,64]{1,3,2,0:T(8,128)(2,1)}, bf16[4,448,3,64]{1,3,2,0:T(8,128)(2,1)}, bf16[4,448,3,64]{1,3,2,0:T(8,128)(2,1)}, bf16[4,4...) while((s32[]{:T(128)}, ...), condition=%wide.region_32.33_spmd.clone.clone, body=%wide.region_30.32_spmd.clone.clone.sunk | while | flops 390827136 | bytes 21527560 | solution.py:289
  1367.1 249.1 %all-reduce.9.cloned.1.call-done = bf16[4,1500,768]{2,0,1:T(4,128)(2,1)} async-done(((bf16[4,1500,768]{2,0,1:T(4,128)(2,1)}), bf16[4,1500,768]{2,0,1:T(4,128)(2,1)}) %all-reduce.9.cloned.1.call-update) | async-done | bytes 9216016
  1627.0 40.7 %all-reduce.6 = (f32[4,768]{1,0:T(4,128)S(1)}, f32[4,768]{1,0:T(4,128)S(1)}, f32[7,768]{1,0:T(8,128)S(1)}, f32[3072]{0:T(1024)S(1)}) all-reduce(f32[4,768]{1,0:T(4,128)S(1)} %pad_maximum_fusion.2, f32[4,768]{1,0:T(4,128)S(1)} %pad_maximum_fusion.3, f32[7,768]{1,0:T(8,128)S(1)} %stack.96, ...), channel_id=16, replica_groups=mesh['fsdp'=8,'tp'=4] {'fsdp','tp'}, use_global_device_ids=true, to_apply=%region_48.49.clone | all-reduce | flops 14592 | bytes 116736
  (542 shorter events, 428.4 us)
Async XLA Ops:
  8.0 141.2 %copy-start.61 = (bf16[192,96]{1,0:T(8,128)(2,1)S(1)}, bf16[192,96]{1,0:T(8,128)(2,1)}, u32[]{:S(2)}) copy-start(bf16[192,96]{1,0:T(8,128)(2,1)} %param.27) | copy-start | bytes 110596
  8.0 141.3 %copy-start.77 = (f32[7,24]{1,0:T(8,128)S(1)}, f32[7,24]{1,0:T(8,128)}, u32[]{:S(2)}) copy-start(f32[7,24]{1,0:T(8,128)} %param.35) | copy-start | bytes 2020
  8.0 221.2 %copy-start.49 = (bf16[3,96,192]{2,1,0:T(8,128)(2,1)S(1)}, bf16[3,96,192]{2,1,0:T(8,128)(2,1)}, u32[]{:S(2)}) copy-start(bf16[3,96,192]{2,1,0:T(8,128)(2,1)} %param.26) | copy-start | bytes 331780
  8.0 233.0 %all-gather.12.cloned.1.call-start = ((), (), s32[]{:S(2)}) async-start(), calls=%async_computation.13 | async-start | bytes 3440640 | tf_op jit(solution)/shard_map/all_gather | solution.py:141
  82.0 301.1 %copy-start.53 = (f32[768]{0:T(1024)}, f32[768]{0:T(1024)S(1)}, u32[]{:S(2)}) copy-start(f32[768]{0:T(1024)S(1)} %get-tuple-element.457) | copy-start | bytes 9220
  149.1 230.9 %reduce-scatter.27.cloned.1.call-start = ((), (), s32[]{:S(2)}) async-start(), calls=%async_computation.14 | async-start | bytes 3440640 | tf_op jit(solution)/shard_map/reduce_scatter | solution.py:145
  229.1 451.5 %copy-start.47 = (f32[768]{0:T(1024)}, f32[768]{0:T(1024)S(1)}, u32[]{:S(2)}) copy-start(f32[768]{0:T(1024)S(1)} %get-tuple-element.558) | copy-start | bytes 9220
  277.5 306.3 %all-gather.14.cloned.1.call-start = ((), (), s32[]{:S(2)}) async-start(), calls=%async_computation.15 | async-start | bytes 3440640 | tf_op jit(solution)/shard_map/all_gather | solution.py:141
  277.5 98.7 %collective-permute-start = (bf16[4,375,768]{2,0,1:T(4,128)(2,1)}, bf16[4,375,768]{2,0,1:T(4,128)(2,1)S(1)}, u32[]{:S(2)}, u32[]{:S(2)}) collective-permute-start(bf16[4,375,768]{2,0,1:T(4,128)(2,1)} %param.24), channel_id=1, source_target_pairs={{0,1},{1,2},{2,3},{3,0},{4,5},{5,6},{6,7},{7,4},{8,9},{9,10},{10,1... | collective-permute-start | bytes 6912008 | tf_op jit(solution)/shard_map/ppermute | solution.py:203
  376.2 91.6 %collective-permute-start.1 = (bf16[4,375,768]{2,0,1:T(4,128)(2,1)S(1)}, bf16[4,375,768]{2,0,1:T(4,128)(2,1)}, u32[]{:S(2)}, u32[]{:S(2)}) collective-permute-start(bf16[4,375,768]{2,0,1:T(4,128)(2,1)S(1)} %collective-permute-done), channel_id=1, source_target_pairs={{0,1},{1,2},{2,3},{3,0},{4,5},{5,6},{6,7},{7,4},{8,9},{9,10},{10,1... | collective-permute-start | bytes 6912008 | tf_op jit(solution)/shard_map/ppermute | solution.py:203
  376.2 145.4 %collective-permute-start.2 = (bf16[4,375,768]{2,0,1:T(4,128)(2,1)}, bf16[4,375,768]{2,0,1:T(4,128)(2,1)}, u32[]{:S(2)}, u32[]{:S(2)}) collective-permute-start(bf16[4,375,768]{2,0,1:T(4,128)(2,1)} %param.24), channel_id=1, source_target_pairs={{0,3},{1,0},{2,1},{3,2},{4,7},{5,4},{6,5},{7,6},{8,11},{9,8},{10,9... | collective-permute-start | bytes 6912008 | tf_op jit(solution)/shard_map/ppermute | solution.py:206
  384.4 296.2 %reduce-scatter.29.cloned.1.call-start = ((), (), s32[]{:S(2)}) async-start(), calls=%async_computation.16 | async-start | bytes 3440640 | tf_op jit(solution)/shard_map/reduce_scatter | solution.py:145
  627.3 102.1 %all-gather.18.cloned.1.call-start = ((), (), s32[]{:S(2)}) async-start(), calls=%async_computation.18 | async-start | bytes 1327104 | tf_op jit(solution)/shard_map/all_gather | solution.py:118
  627.9 114.2 %all-gather.16.cloned.1.call-start = ((), (), s32[]{:S(2)}) async-start(), calls=%async_computation.17 | async-start | bytes 3440640 | tf_op jit(solution)/shard_map/all_gather | solution.py:141
  684.6 81.9 %all-gather.20.cloned.1.call-start = ((), (), s32[]{:S(2)}) async-start(), calls=%async_computation.19 | async-start | bytes 1327104 | tf_op jit(solution)/shard_map/all_gather | solution.py:119
  685.2 141.7 %reduce-scatter.31.cloned.1.call-start = ((), (), s32[]{:S(2)}) async-start(), calls=%async_computation.20 | async-start | bytes 3440640 | tf_op jit(solution)/shard_map/reduce_scatter | solution.py:145
  772.5 116.2 %all-gather.22.cloned.1.call-start = ((), (), s32[]{:S(2)}) async-start(), calls=%async_computation.21 | async-start | bytes 3440640 | tf_op jit(solution)/shard_map/all_gather | solution.py:153
  832.2 123.6 %reduce-scatter.33.cloned.1.call-start = ((), (), s32[]{:S(2)}) async-start(), calls=%async_computation.22 | async-start | bytes 3440640 | tf_op jit(solution)/shard_map/reduce_scatter | solution.py:157
  902.6 116.8 %all-gather.24.cloned.1.call-start = ((), (), s32[]{:S(2)}) async-start(), calls=%async_computation.23 | async-start | bytes 3440640 | tf_op jit(solution)/shard_map/all_gather | solution.py:153
  962.7 174.8 %reduce-scatter.35.cloned.1.call-start = ((), (), s32[]{:S(2)}) async-start(), calls=%async_computation.24 | async-start | bytes 3440640 | tf_op jit(solution)/shard_map/reduce_scatter | solution.py:157
  1084.3 181.2 %all-gather.26.cloned.1.call-start = ((), (), s32[]{:S(2)}) async-start(), calls=%async_computation.25 | async-start | bytes 3440640 | tf_op jit(solution)/shard_map/all_gather | solution.py:153
  1142.7 221.0 %reduce-scatter.51.cloned.1.call-start = ((), (), s32[]{:S(2)}) async-start(), calls=%async_computation.33 | async-start | bytes 884736
  1166.1 199.2 %reduce-scatter.49.cloned.1.call-start = ((), (), s32[]{:S(2)}) async-start(), calls=%async_computation.32 | async-start | bytes 1327104
  1194.0 422.2 %all-reduce.9.cloned.1.call-start = ((), (), s32[]{:S(2)}) async-start(), calls=%async_computation.34 | async-start | bytes 18432000
  1265.0 356.5 %reduce-scatter.45.cloned.1.call-start = ((), (), s32[]{:S(2)}) async-start(), calls=%async_computation.30 | async-start | bytes 884736
  1316.8 306.4 %reduce-scatter.43.cloned.1.call-start = ((), (), s32[]{:S(2)}) async-start(), calls=%async_computation.29 | async-start | bytes 2211840
  1337.1 288.0 %reduce-scatter.37.cloned.1.call-start = ((), (), s32[]{:S(2)}) async-start(), calls=%async_computation.26 | async-start | bytes 3440640 | tf_op jit(solution)/shard_map/reduce_scatter | solution.py:157
  1341.9 331.5 %reduce-scatter.39.cloned.1.call-start = ((), (), s32[]{:S(2)}) async-start(), calls=%async_computation.27 | async-start | bytes 2654208 | tf_op jit(solution)/shard_map/reduce_scatter | solution.py:356
  1348.7 324.7 %reduce-scatter.41.cloned.1.call-start = ((), (), s32[]{:S(2)}) async-start(), calls=%async_computation.28 | async-start | bytes 2654208 | tf_op jit(solution)/shard_map/reduce_scatter | solution.py:357
  1355.6 317.8 %reduce-scatter.47.cloned.1.call-start = ((), (), s32[]{:S(2)}) async-start(), calls=%async_computation.31 | async-start | bytes 884736
  1367.1 253.5 %copy-start.18 = (bf16[4,448,3,64]{1,3,2,0:T(8,128)(2,1)S(1)}, bf16[4,448,3,64]{1,3,2,0:T(8,128)(2,1)}, u32[]{:S(2)}) copy-start(bf16[4,448,3,64]{1,3,2,0:T(8,128)(2,1)} %get-tuple-element.211) | copy-start | bytes 2064388
  1367.1 253.7 %copy-start.20 = (bf16[4,448,3,64]{1,3,2,0:T(8,128)(2,1)S(1)}, bf16[4,448,3,64]{1,3,2,0:T(8,128)(2,1)}, u32[]{:S(2)}) copy-start(bf16[4,448,3,64]{1,3,2,0:T(8,128)(2,1)} %get-tuple-element.209) | copy-start | bytes 2064388
  (86 other events, 1582.8 us)
Sparse Core Ops, SparseCore 0:
  149.2 56.4 all-gather.11
  277.6 96.7 reduce-scatter.26
  384.5 111.7 all-gather.13
  627.4 53.1 reduce-scatter.28
  962.9 56.5 all-gather.23
  1084.5 53.0 reduce-scatter.34
  1265.1 351.0 all-reduce.8
Sparse Core Ops, SparseCore 1:
  629.7 22.6 all-gather.17
  684.7 57.4 all-gather.15
  743.9 22.5 all-gather.19
  772.5 54.3 reduce-scatter.30
  832.2 56.3 all-gather.21
  902.7 53.0 reduce-scatter.32
  1142.7 56.4 all-gather.25
  1202.2 33.6 reduce-scatter.50
  1238.9 36.7 reduce-scatter.48
  1316.8 34.5 reduce-scatter.44
  1354.7 40.1 reduce-scatter.42
  1397.2 120.1 reduce-scatter.36
  1521.1 42.2 reduce-scatter.38
  1567.3 42.2 reduce-scatter.40
  1613.3 35.0 reduce-scatter.46
